TPU v7x, 32 devices: a whole 2x2x4 slice. The times are simulated.
32 devices in a mesh: grid: 8 (over z, y), tile: 4 (over x, core).
Axes of the slice: x: 2, y: 2, z: 4, core: 2. Of those that a mesh axis runs over, the one named last changes fastest.
Arguments:
- point_values: bfloat16 [256, 16384], P('grid', 'tile'), may hold values from -1.75 to 1.75
- sig_blocks: int32 [8, 16], P('grid'), may hold values from 0 to 31, as said below
- density: bfloat16 [16384, 16384], P('grid', 'tile'), may hold values from -0.0625 to 0.0625
- coulomb_core: bfloat16 [512, 512], replicated, may hold values from -0.25 to 0.25
- screen_mask: int32 [32, 32], replicated, may hold values 0 or 1
- ao_centers: float32 [3, 16384], replicated, may hold values from -1 to 1
- ao_widths: float32 [16384], replicated, may hold values from 0.25 to 1
- point_coords: float32 [3, 256], P(None, 'grid'), may hold values from -1 to 1
- lmo_coeffs: bfloat16 [16384, 1024], P('tile'), may hold values from -0.0625 to 0.0625
- domain_blocks: int32 [4, 16], replicated, may hold values from 0 to 31, as said below
Outputs:
- half: bfloat16 [1024, 16384], P('tile', 'grid')
Inputs may be any that keep to these rules, and one draw needn't show every extreme that they name: `sig_blocks`: each batch names 16 different AO blocks. `domain_blocks`: each strip's 16 blocks are different, and every AO block lies in the domain of some strip.
All inputs are finite; a program needn't handle non-finite values.
Results may differ from a plain program's by a relative error of at most 0.02.
Values may be sent and summed in bfloat16 or wider, within the bound.
A program may use at most 128 MiB of HBM per device.

v0:
```python
import jax
import jax.numpy as jnp
from jax import lax
from jax.sharding import PartitionSpec as P

highest = lax.Precision.HIGHEST


def kernel_weights(ao_centers, ao_widths, point_coords):
    offsets = ao_centers[:, None, :] - point_coords[:, :, None]
    return 1.0 / jnp.sqrt(jnp.sum(offsets * offsets, axis=0) + ao_widths[None, :])


def spread_mask(flag_rows, batch_points, block_size):
    batches, block_count = flag_rows.shape
    expanded = jnp.broadcast_to(
        flag_rows[:, None, :, None], (batches, batch_points, block_count, block_size)
    )
    return expanded.reshape(batches * batch_points, block_count * block_size)


def shards(
    point_values,
    sig_blocks,
    density,
    coulomb_core,
    screen_mask,
    ao_centers,
    ao_widths,
    point_coords,
    lmo_coeffs,
    domain_blocks,
):
    grid_count = lax.axis_size("grid")
    panel_index = lax.axis_index("tile")
    batches = sig_blocks.shape[0]
    own_rows, own_cols = density.shape
    points = point_values.shape[0]
    batch_points = points // batches
    block_size = coulomb_core.shape[0]
    total_aos = ao_widths.shape[0]
    all_blocks = total_aos // block_size
    col_blocks = own_cols // block_size
    row_blocks = own_rows // block_size
    block_ids = jnp.arange(all_blocks, dtype=jnp.int32)
    named_blocks = jnp.any(sig_blocks[:, :, None] == block_ids[None, None, :], axis=1).astype(
        jnp.float32
    )
    first_col = panel_index * col_blocks
    named_cols = lax.dynamic_slice_in_dim(named_blocks, first_col, col_blocks, 1)
    col_mask = spread_mask(named_cols, batch_points, block_size)
    masked_local = point_values * col_mask.astype(jnp.bfloat16)
    dest_named = jnp.max(named_blocks.reshape(batches, grid_count, row_blocks), axis=2)
    outgoing = masked_local.reshape(batches, batch_points, 1, own_cols) * dest_named[
        :, None, :, None
    ].astype(jnp.bfloat16)
    product = jnp.einsum(
        "bpgc,rc->bpgr",
        lax.all_to_all(outgoing, "grid", split_axis=2, concat_axis=2, tiled=True),
        density,
        preferred_element_type=jnp.float32,
    )
    arrivals = lax.all_to_all(
        product.astype(jnp.bfloat16), "grid", split_axis=2, concat_axis=2, tiled=True
    )
    row_mask = spread_mask(named_blocks, batch_points, block_size)
    partial_term = arrivals.reshape(points, total_aos).astype(jnp.float32) * row_mask
    coefficient = kernel_weights(ao_centers, ao_widths, point_coords)
    core_float = coulomb_core.astype(jnp.float32)
    screen_float = screen_mask.astype(jnp.float32)
    density_term = lax.psum(partial_term.astype(jnp.bfloat16), "tile").astype(jnp.float32)
    weighted = (coefficient * density_term).reshape(points, all_blocks, block_size)
    screen_rows = lax.dynamic_slice_in_dim(screen_float, first_col, col_blocks, 0)
    screened = jnp.einsum("kj,pja->pka", screen_rows, weighted, precision=highest)
    kernel_part = jnp.einsum(
        "ab,pkb->pka", core_float, screened, preferred_element_type=jnp.float32
    ).reshape(points, own_cols)
    coeff_cols = lax.dynamic_slice_in_dim(coefficient, panel_index * own_cols, own_cols, 1)
    potential = (coeff_cols * kernel_part * col_mask).astype(jnp.bfloat16)
    potential_out = jnp.broadcast_to(
        potential.reshape(batches, batch_points, 1, own_cols),
        (batches, batch_points, grid_count, own_cols),
    )
    whole_points = lax.all_gather(masked_local, "tile", axis=1, tiled=True)
    row_values, col_values = (
        lax.all_to_all(
            whole_points.reshape(batches, batch_points, grid_count, own_rows),
            "grid",
            split_axis=2,
            concat_axis=2,
            tiled=True,
        ),
        lax.all_to_all(potential_out, "grid", split_axis=2, concat_axis=2, tiled=True),
    )
    exch_tile = jnp.einsum(
        "bpgr,bpgc->rc", row_values, col_values, preferred_element_type=jnp.float32
    ).astype(jnp.bfloat16)
    number_of_slabs = domain_blocks.shape[0]
    localized_orbital_total = lmo_coeffs.shape[1]
    strip_width = localized_orbital_total // number_of_slabs
    local_ids = first_col + jnp.arange(col_blocks, dtype=jnp.int32)
    in_domain = jnp.any(domain_blocks[:, :, None] == local_ids[None, None, :], axis=1)
    domain_flags = jnp.transpose(in_domain)
    domain_mask = jnp.broadcast_to(
        domain_flags[:, None, :, None], (col_blocks, block_size, number_of_slabs, strip_width)
    ).reshape(own_cols, localized_orbital_total)
    region_expansion_factor = lmo_coeffs * domain_mask.astype(jnp.bfloat16)
    return lax.psum_scatter(
        lax.dot_general(
            region_expansion_factor,
            exch_tile,
            (((0,), (1,)), ((), ())),
            preferred_element_type=jnp.float32,
        ).astype(jnp.bfloat16),
        "tile",
        scatter_dimension=0,
        tiled=True,
    )


def solution(mesh):
    in_specs = (
        P("grid", "tile"),
        P("grid", None),
        P("grid", "tile"),
        P(),
        P(),
        P(),
        P(),
        P(None, "grid"),
        P("tile", None),
        P(),
    )
    out_specs = P("tile", "grid")
    return jax.shard_map(shards, mesh=mesh, in_specs=in_specs, out_specs=out_specs, check_vma=False)
```

profile of v0, /device:TPU:0, one launch (start us, length us, event | category | flops | bytes accessed | tf_op | source)
XLA Modules:
  0.0 288.2 jit_solution(9041671634119760462)
XLA Ops:
  6.5 0.0 copy-start
  6.5 0.8 fusion.26
  7.3 0.1 reshape.142
  7.4 0.1 dynamic-slice.3
  7.5 0.1 broadcast_bitcast_fusion.1
  7.6 0.1 reduce_max.9
  7.7 1.0 broadcast_multiply_fusion.1
  8.7 0.0 copy-start.2
  8.7 0.2 broadcast_multiply_fusion
  8.9 55.3 %all_to_all.20 = bf16[1,32,8,4096]{3,1,0,2:T(8,128)(2,1)S(1)} all-to-all(bf16[1,32,8,4096]{3,1,0,2:T(8,128)(2,1)S(1)} %broadcast_multiply_fusion), channel_id=1, replica_groups=mesh['grid'=8,'tile'=4] {'grid'}, dimensions={2} | all-to-all | bytes 4194304 | tf_op jit(solution)/shard_map/all_to_all | solution.py:59
  64.3 0.0 copy-done.2
  64.3 9.6 %fusion.11 = bf16[1,32,8,2048]{3,2,1,0:T(8,128)(2,1)} fusion(bf16[2048,4096]{1,0:T(8,128)(2,1)} %param.12, bf16[1,32,8,4096]{3,1,0,2:T(8,128)(2,1)S(1)} %all_to_all.20), kind=kOutput, calls=%fused_computation.9 | convolution fusion | flops 4295491584 | bytes 19922944 | tf_op jit(solution)/shard_map/bpgc,rc->bpgr/dot_general | solution.py:57
  73.8 2.8 copy.25
  76.6 3.6 %all-to-all-start.2 = ((bf16[1,32,8,2048]{3,1,0,2:T(8,128)(2,1)}), bf16[1,32,8,2048]{3,1,0,2:T(8,128)(2,1)S(1)}, u32[]{:S(2)}, u32[]{:S(2)}) async-start(bf16[1,32,8,2048]{3,1,0,2:T(8,128)(2,1)} %copy.25), calls=%async_computation.2 | async-start | bytes 2097152 | tf_op jit(solution)/shard_map/all_to_all | solution.py:63
  80.2 0.0 all-gather.2.cloned.1.call-start
  80.2 0.7 all-gather.2.cloned.1.call-update
  80.9 0.0 all-reduce.2.cloned.1.call-start
  81.0 0.1 broadcast_bitcast_fusion
  81.1 24.7 %all-to-all-done.2 = bf16[1,32,8,2048]{3,1,0,2:T(8,128)(2,1)S(1)} async-done(((bf16[1,32,8,2048]{3,1,0,2:T(8,128)(2,1)}), bf16[1,32,8,2048]{3,1,0,2:T(8,128)(2,1)S(1)}, u32[]{:S(2)}, u32[]{:S(2)}) %all-to-all-start.2) | async-done | bytes 1048608 | tf_op jit(solution)/shard_map/all_to_all | solution.py:63
  105.8 0.2 copy.31
  106.0 0.0 copy-start.3
  106.0 0.0 copy-start.6
  106.0 1.1 multiply_convert_fusion
  107.2 0.0 all-reduce.2.cloned.1.call-update
  107.2 0.0 copy-done.3
  107.2 0.0 copy-done.6
  107.2 0.8 multiply_reduce_fusion
  108.0 0.0 all-gather.2.cloned.1.call-done
  108.0 1.8 copy.30
  109.8 0.0 copy-start.4
  109.9 1.6 copy.22
  111.5 4.2 %all-to-all-start = ((bf16[1,32,8,2048]{3,1,0,2:T(8,128)(2,1)}), bf16[1,32,8,2048]{3,1,0,2:T(8,128)(2,1)}, u32[]{:S(2)}, u32[]{:S(2)}) async-start(bf16[1,32,8,2048]{3,1,0,2:T(8,128)(2,1)} %copy.22), calls=%async_computation | async-start | bytes 2097152 | tf_op jit(solution)/shard_map/all_to_all | solution.py:86
  115.7 26.8 %all-reduce.2.cloned.1.call-done = bf16[32,16384]{1,0:T(8,128)(2,1)} async-done(((bf16[32,16384]{1,0:T(8,128)(2,1)}), bf16[32,16384]{1,0:T(8,128)(2,1)}) %all-reduce.2.cloned.1.call-update) | async-done | bytes 1048592 | tf_op jit(solution)/shard_map/psum | solution.py:71
  142.5 0.0 copy-done.4
  142.5 1.5 convert_multiply_fusion
  144.0 1.2 copy.33
  145.2 1.9 convolution_bitcast_fusion
  147.1 0.0 copy-done
  147.1 0.3 fusion.24
  147.5 0.3 copy.34
  147.8 0.1 multiply_convert_fusion.1
  147.9 0.0 all-to-all-done
  147.9 1.6 broadcast_in_dim.49
  149.5 0.0 copy-start.5
  149.5 5.9 %all-to-all-start.3 = ((bf16[1,32,8,4096]{3,1,0,2:T(8,128)(2,1)}), bf16[1,32,8,4096]{3,1,0,2:T(8,128)(2,1)S(1)}, u32[]{:S(2)}, u32[]{:S(2)}) async-start(bf16[1,32,8,4096]{3,1,0,2:T(8,128)(2,1)} %broadcast_in_dim.49), calls=%async_computation.3 | async-start | bytes 4194304 | tf_op jit(solution)/shard_map/all_to_all | solution.py:93
  155.4 0.2 reduce-scatter.2.cloned.1.call-start
  155.6 0.0 copy-done.5
  155.7 0.2 compare_reduce_fusion
  155.9 0.1 copy.21
  156.0 2.2 broadcast_in_dim.18
  158.2 4.0 %copy.28 = pred[512,8,4,256]{3,1,2,0:T(8,128)(4,1)} copy(pred[512,8,4,256]{3,2,1,0:T(4,128)(4,1)S(1)} %bitcast.72) | data formatting | bytes 8388608
  162.3 40.5 %all-to-all-done.3 = bf16[1,32,8,4096]{3,1,0,2:T(8,128)(2,1)S(1)} async-done(((bf16[1,32,8,4096]{3,1,0,2:T(8,128)(2,1)}), bf16[1,32,8,4096]{3,1,0,2:T(8,128)(2,1)S(1)}, u32[]{:S(2)}, u32[]{:S(2)}) %all-to-all-start.3) | async-done | bytes 2097184 | tf_op jit(solution)/shard_map/all_to_all | solution.py:93
  202.8 10.0 %bitcast_convert_fusion.clone.7 = bf16[2048,4096]{1,0:T(8,128)(2,1)} fusion(bf16[1,32,8,4096]{3,1,0,2:T(8,128)(2,1)S(1)} %all-to-all-done.3, bf16[1,32,8,2048]{3,1,0,2:T(8,128)(2,1)} %all-to-all-done), kind=kOutput, calls=%fused_computation.clone.clone.clone.clone.clone.2 | convolution fusion | flops 4303355904 | bytes 19922944 | tf_op jit(solution)/shard_map/bpgr,bpgc->rc/dot_general | solution.py:95
  212.8 25.2 %fusion.5 = bf16[1024,2048]{1,0:T(8,128)(2,1)} fusion(pred[4096,1024]{1,0:T(8,128)(4,1)} %bitcast.77, bf16[4096,1024]{1,0:T(8,128)(2,1)} %param.18, bf16[2048,4096]{1,0:T(8,128)(2,1)} %bitcast_convert_fusion.clone.7), kind=kOutput, calls=%fused_computation.7 | convolution fusion | flops 17186160640 | bytes 33554432 | tf_op jit(solution)/shard_map/dot_general | solution.py:109
  237.9 0.0 copy-start.1
  237.9 0.0 reduce-scatter.2.cloned.1.call-update
  237.9 43.7 %reduce-scatter.2.cloned.1.call-done = bf16[256,2048]{1,0:T(8,128)(2,1)} async-done(((bf16[1024,2048]{1,0:T(8,128)(2,1)}), bf16[256,2048]{1,0:T(8,128)(2,1)}) %reduce-scatter.2.cloned.1.call-update) | async-done | bytes 1048592 | tf_op jit(solution)/shard_map/reduce_scatter | solution.py:108
  281.6 0.0 copy-done.1
  (5 shorter events, 0.0 us)
Async XLA Ops:
  6.5 140.6 %copy-start = (bf16[512,512]{1,0:T(8,128)(2,1)S(1)}, bf16[512,512]{1,0:T(8,128)(2,1)}, u32[]{:S(2)}) copy-start(bf16[512,512]{1,0:T(8,128)(2,1)} %param.13) | copy-start | bytes 1572868
  8.7 55.6 %copy-start.2 = (bf16[32,4096]{1,0:T(8,128)(2,1)}, bf16[32,4096]{1,0:T(8,128)(2,1)S(1)}, u32[]{:S(2)}) copy-start(bf16[32,4096]{1,0:T(8,128)(2,1)S(1)} %broadcast_multiply_fusion.1) | copy-start | bytes 786436
  76.6 29.2 %all-to-all-start.2 = ((bf16[1,32,8,2048]{3,1,0,2:T(8,128)(2,1)}), bf16[1,32,8,2048]{3,1,0,2:T(8,128)(2,1)S(1)}, u32[]{:S(2)}, u32[]{:S(2)}) async-start(bf16[1,32,8,2048]{3,1,0,2:T(8,128)(2,1)} %copy.25), calls=%async_computation.2 | async-start | bytes 2097152 | tf_op jit(solution)/shard_map/all_to_all | solution.py:63
  80.2 27.8 %all-gather.2.cloned.1.call-start = ((), (), s32[]{:S(2)}) async-start(), calls=%async_computation.5 | async-start | bytes 1310720 | tf_op jit(solution)/shard_map/all_gather | solution.py:84
  80.9 61.6 %all-reduce.2.cloned.1.call-start = ((), (), s32[]{:S(2)}) async-start(), calls=%async_computation.6 | async-start | bytes 2097152 | tf_op jit(solution)/shard_map/psum | solution.py:71
  106.0 1.2 copy-start.3
  106.0 1.2 copy-start.6
  109.8 32.6 %copy-start.4 = (f32[16384]{0:T(1024)S(1)}, f32[16384]{0:T(1024)}, u32[]{:S(2)}) copy-start(f32[16384]{0:T(1024)} %param.16) | copy-start | bytes 196612
  111.5 36.4 %all-to-all-start = ((bf16[1,32,8,2048]{3,1,0,2:T(8,128)(2,1)}), bf16[1,32,8,2048]{3,1,0,2:T(8,128)(2,1)}, u32[]{:S(2)}, u32[]{:S(2)}) async-start(bf16[1,32,8,2048]{3,1,0,2:T(8,128)(2,1)} %copy.22), calls=%async_computation | async-start | bytes 2097152 | tf_op jit(solution)/shard_map/all_to_all | solution.py:86
  149.5 6.2 %copy-start.5 = (s32[4,16]{1,0:T(4,128)S(1)}, s32[4,16]{1,0:T(4,128)}, u32[]{:S(2)}) copy-start(s32[4,16]{1,0:T(4,128)} %param.19) | copy-start | bytes 772
  149.5 53.3 %all-to-all-start.3 = ((bf16[1,32,8,4096]{3,1,0,2:T(8,128)(2,1)}), bf16[1,32,8,4096]{3,1,0,2:T(8,128)(2,1)S(1)}, u32[]{:S(2)}, u32[]{:S(2)}) async-start(bf16[1,32,8,4096]{3,1,0,2:T(8,128)(2,1)} %broadcast_in_dim.49), calls=%async_computation.3 | async-start | bytes 4194304 | tf_op jit(solution)/shard_map/all_to_all | solution.py:93
  155.4 126.2 %reduce-scatter.2.cloned.1.call-start = ((), (), s32[]{:S(2)}) async-start(), calls=%async_computation.7 | async-start | bytes 5242880 | tf_op jit(solution)/shard_map/reduce_scatter | solution.py:108
  237.9 43.7 %copy-start.1 = (bf16[512,512]{1,0:T(8,128)(2,1)S(1)}, bf16[512,512]{1,0:T(8,128)(2,1)}, u32[]{:S(2)}) copy-start(bf16[512,512]{1,0:T(8,128)(2,1)} %param.13) | copy-start | bytes 1572868
Sparse Core Ops, SparseCore 0:
  82.6 18.0 all-gather.1
  107.3 35.1 all-reduce.1
  238.1 43.5 reduce-scatter.1
where the time goes:
time: 289 us; the launch traced here: 288 us
  waiting for transfers between devices  136 us (47%)
  blocking collectives  55.3 us (19%)
  matrix products  46.9 us (16%)
  local copies, waits for them, and re-layouts  16.3 us (6%)
  starting transfers between devices  14 us (5%)
  between operations  13.3 us (5%)
  other arithmetic  5.85 us (2%)
    all_to_all x1, blocking collectives, shards(): lax.all_to_all(outgoing, 'grid', split_axis=2, concat_axis=2, tiled=True)  55.3 us
    reduce_scatter x1, waiting for transfers between devices, shards(): lax.psum_scatter(lax.dot_general(region_expansion_factor, exch_tile, (((0...  43.7 us
    all_to_all x1, waiting for transfers between devices, shards(): lax.all_to_all(potential_out, 'grid', split_axis=2, concat_axis=2, tiled=...  40.5 us
    psum x1, waiting for transfers between devices, shards(): lax.psum(partial_term.astype(jnp.bfloat16), 'tile').astype(jnp.float32)  26.8 us
    dot_general x1, matrix products, shards(): lax.dot_general(region_expansion_factor, exch_tile, (((0,), (1,)), ((), (...  25.2 us
    all_to_all x1, waiting for transfers between devices, shards(): lax.all_to_all(product.astype(jnp.bfloat16), 'grid', split_axis=2, concat...  24.7 us
    dot_general x1, matrix products, shards(): jnp.einsum('bpgr,bpgc->rc', row_values, col_values, preferred_element_typ...  9.96 us
    dot_general x1, matrix products, shards(): jnp.einsum('bpgc,rc->bpgr', lax.all_to_all(outgoing, 'grid', split_axis=2...  9.56 us
  transfers between devices with their start and end apart: 6, of which 4 were waited for; matrix products, arithmetic and copies ran while one was open for 6% of the time, Pallas kernels for 0%

commit v1 on v0

--- a/solution.py
+++ b/solution.py
@@ -4,6 +4,21 @@
 from jax.sharding import PartitionSpec as P
 
 highest = lax.Precision.HIGHEST
+
+
+def _derive_blocks(view, in_dim, array_in):
+    vec_out, passed = (view.shape[:in_dim], view.shape[in_dim + 1 :])
+    d_next = jnp.moveaxis(view.reshape(*vec_out, array_in, -1, *passed), in_dim, 0)
+    return d_next
+
+
+def treat_goods(x_local, on_dim):
+    x_local = jnp.moveaxis(x_local, 0, on_dim)
+    work_now = x_local.shape
+    formed = x_local.reshape(
+        *work_now[:on_dim], work_now[on_dim] * work_now[on_dim + 1], *work_now[on_dim + 2 :]
+    )
+    return formed
 
 
 def kernel_weights(ao_centers, ao_widths, point_coords):
@@ -60,9 +75,22 @@
         density,
         preferred_element_type=jnp.float32,
     )
-    arrivals = lax.all_to_all(
-        product.astype(jnp.bfloat16), "grid", split_axis=2, concat_axis=2, tiled=True
-    )
+
+    def see_runs(x0, group_axis, block_in, load):
+        x_now, shaped = (lax.axis_size(group_axis), lax.axis_index(group_axis))
+        w_next = _derive_blocks(x0, block_in, x_now)
+        clean = w_next
+        for dev_i in range(1, x_now):
+            fresh, e_now = ((shaped + dev_i) % x_now, (shaped - dev_i) % x_now)
+            y2 = lax.dynamic_index_in_dim(w_next, fresh, 0)
+            f_next = lax.ppermute(
+                y2, group_axis, [(j0, (j0 + dev_i) % x_now) for j0 in range(x_now)]
+            )
+            clean = lax.dynamic_update_slice_in_dim(clean, f_next, e_now, axis=0)
+        value_now = treat_goods(clean, load)
+        return value_now
+
+    arrivals = see_runs(product.astype(jnp.bfloat16), group_axis="grid", block_in=2, load=2)
     row_mask = spread_mask(named_blocks, batch_points, block_size)
     partial_term = arrivals.reshape(points, total_aos).astype(jnp.float32) * row_mask
     coefficient = kernel_weights(ao_centers, ao_widths, point_coords)

time: 289 us -> 322 us (1.11)
  blocking collectives: 55.3 us -> 0 us
  waiting for transfers between devices: 136 us -> 186 us
  starting transfers between devices: 14 us -> 34.6 us
  local copies, waits for them, and re-layouts: 16.3 us -> 31.4 us
    all_to_all x1 -> x0, blocking collectives: 55.3 us -> none  [shards(): lax.all_to_all(outgoing, 'grid', split_axis=2, concat_axis=2, tiled=True)]
    ppermute x0 -> x7, waiting for transfers between devices: none -> 27.9 us  [see_runs(): lax.ppermute(y2, group_axis, [(j0, (j0 + dev_i) % x_now) for j0 in range(...]
    all_to_all x1, waiting for transfers between devices: 24.7 us -> 48.2 us  [shards(): lax.all_to_all(outgoing, 'grid', split_axis=2, concat_axis=2, tiled=True)]
    ppermute x0 -> x7, starting transfers between devices: none -> 17.1 us  [see_runs(): lax.ppermute(y2, group_axis, [(j0, (j0 + dev_i) % x_now) for j0 in range(...]
    dynamic_update_slice x0 -> x7, local copies, waits for them, and re-layouts: none -> 14.1 us  [see_runs(): clean = lax.dynamic_update_slice_in_dim(clean, f_next, e_now, axis=0)]
    all_to_all x1, starting transfers between devices: 3.59 us -> 7.31 us  [shards(): lax.all_to_all(outgoing, 'grid', split_axis=2, concat_axis=2, tiled=True)]
  transfers between devices with their start and end apart: 6 -> 13, of which waited for: 4 -> 6; matrix products, arithmetic and copies ran while one was open for 6% -> 10% of each run, Pallas kernels for 0% -> 0%
where the time goes in v1:
time: 322 us
  waiting for transfers between devices  186 us (58%)
  matrix products  48.9 us (15%)
  starting transfers between devices  34.6 us (11%)
  local copies, waits for them, and re-layouts  31.4 us (10%)
  between operations  13.7 us (4%)
  other arithmetic  7.39 us (2%)
    all_to_all x1, waiting for transfers between devices, shards(): lax.all_to_all(outgoing, 'grid', split_axis=2, concat_axis=2, tiled=True)  48.2 us
    reduce_scatter x1, waiting for transfers between devices, shards(): lax.psum_scatter(lax.dot_general(region_expansion_factor, exch_tile, (((0...  43.6 us
    all_to_all x1, waiting for transfers between devices, shards(): lax.all_to_all(potential_out, 'grid', split_axis=2, concat_axis=2, tiled=...  40.6 us
    ppermute x7, waiting for transfers between devices, see_runs(): lax.ppermute(y2, group_axis, [(j0, (j0 + dev_i) % x_now) for j0 in range(...  27.9 us
    psum x1, waiting for transfers between devices, shards(): lax.psum(partial_term.astype(jnp.bfloat16), 'tile').astype(jnp.float32)  25.5 us
    dot_general x1, matrix products, shards(): lax.dot_general(region_expansion_factor, exch_tile, (((0,), (1,)), ((), (...  25.2 us
    ppermute x7, starting transfers between devices, see_runs(): lax.ppermute(y2, group_axis, [(j0, (j0 + dev_i) % x_now) for j0 in range(...  17.1 us
    dynamic_update_slice x7, local copies, waits for them, and re-layouts, see_runs(): clean = lax.dynamic_update_slice_in_dim(clean, f_next, e_now, axis=0)  14.1 us
  transfers between devices with their start and end apart: 13, of which 6 were waited for; matrix products, arithmetic and copies ran while one was open for 10% of the time, Pallas kernels for 0%

profile of v1, /device:TPU:0, one launch (start us, length us, event | category | flops | bytes accessed | tf_op | source)
XLA Modules:
  0.0 321.8 jit_solution(17234974939090938909)
XLA Ops:
  6.5 0.8 fusion.23
  7.3 0.1 reshape.167
  7.4 0.1 dynamic-slice.31
  7.5 0.1 broadcast_bitcast_fusion.1
  7.6 0.1 reduce_max.9
  7.7 1.0 broadcast_multiply_fusion.1
  8.7 1.5 broadcast_multiply_fusion
  10.2 7.3 %all-to-all-start.1 = ((bf16[1,32,8,4096]{3,1,0,2:T(8,128)(2,1)}), bf16[1,32,8,4096]{3,1,0,2:T(8,128)(2,1)}, u32[]{:S(2)}, u32[]{:S(2)}) async-start(bf16[1,32,8,4096]{3,1,0,2:T(8,128)(2,1)} %broadcast_multiply_fusion), calls=%async_computation.1 | async-start | bytes 4194304 | tf_op jit(solution)/shard_map/all_to_all | solution.py:74
  17.5 0.0 all-gather.2.cloned.1.call-start
  17.7 48.2 %all-to-all-done.1 = bf16[1,32,8,4096]{3,1,0,2:T(8,128)(2,1)} async-done(((bf16[1,32,8,4096]{3,1,0,2:T(8,128)(2,1)}), bf16[1,32,8,4096]{3,1,0,2:T(8,128)(2,1)}, u32[]{:S(2)}, u32[]{:S(2)}) %all-to-all-start.1) | async-done | bytes 2097184 | tf_op jit(solution)/shard_map/all_to_all | solution.py:74
  65.9 11.5 %fusion.8 = bf16[32,8,2048]{2,1,0:T(8,128)(2,1)S(1)} fusion(bf16[2048,4096]{1,0:T(8,128)(2,1)} %param.12, bf16[1,32,8,4096]{3,1,0,2:T(8,128)(2,1)} %all-to-all-done.1), kind=kOutput, calls=%fused_computation.8 | convolution fusion | flops 4295491584 | bytes 19922944 | tf_op jit(solution)/shard_map/bpgc,rc->bpgr/dot_general | solution.py:72
  77.4 2.9 dynamic-slice_bitcast_fusion
  80.3 0.0 collective-permute-start.1
  80.3 1.5 collective-permute-start
  81.7 0.0 all-gather.2.cloned.1.call-update
  81.8 0.0 all-reduce.2.cloned.1.call-start
  81.9 3.3 %collective-permute-start.6 = (bf16[1,1,32,1,2048]{4,0,2,3,1:T(2,128)(2,1)}, bf16[1,1,32,1,2048]{4,0,2,3,1:T(2,128)(2,1)S(1)}, u32[]{:S(2)}, u32[]{:S(2)}) collective-permute-start(bf16[1,1,32,1,2048]{4,0,2,3,1:T(2,128)(2,1)} %get-tuple-element.7), channel_id=1, source_target_pairs={{0,28},{4,0},{8,4},{12,8},{16,12},{20,16},{24,20},{28,24},{1,29},{... | collective-permute-start | bytes 393224 | tf_op jit(solution)/shard_map/ppermute | solution.py:86
  85.2 2.0 collective-permute-start.5
  87.3 4.0 %collective-permute-done.1 = bf16[1,1,32,1,2048]{4,0,2,3,1:T(2,128)(2,1)S(1)} collective-permute-done((bf16[1,1,32,1,2048]{4,0,2,3,1:T(2,128)(2,1)S(1)}, bf16[1,1,32,1,2048]{4,0,2,3,1:T(2,128)(2,1)S(1)}, u32[]{:S(2)}, u32[]{:S(2)}) %collective-permute-start.1) | collective-permute-done | bytes 131104 | tf_op jit(solution)/shard_map/ppermute | solution.py:86
  91.2 10.3 %collective-permute-start.3 = (bf16[1,1,32,1,2048]{4,0,2,3,1:T(2,128)(2,1)}, bf16[1,1,32,1,2048]{4,0,2,3,1:T(2,128)(2,1)S(1)}, u32[]{:S(2)}, u32[]{:S(2)}) collective-permute-start(bf16[1,1,32,1,2048]{4,0,2,3,1:T(2,128)(2,1)} %get-tuple-element.10), channel_id=1, source_target_pairs={{0,16},{4,20},{8,24},{12,28},{16,0},{20,4},{24,8},{28,12},{1,17},{... | collective-permute-start | bytes 393224 | tf_op jit(solution)/shard_map/ppermute | solution.py:86
  101.5 0.0 collective-permute-done
  101.5 0.0 collective-permute-start.2
  101.5 0.1 broadcast_bitcast_fusion
  101.6 2.0 dynamic_update_slice.21
  103.7 2.0 dynamic_update_slice.22
  105.7 23.9 %collective-permute-done.2 = bf16[1,1,32,1,2048]{4,0,2,3,1:T(2,128)(2,1)S(1)} collective-permute-done((bf16[1,1,32,1,2048]{4,0,2,3,1:T(2,128)(2,1)}, bf16[1,1,32,1,2048]{4,0,2,3,1:T(2,128)(2,1)S(1)}, u32[]{:S(2)}, u32[]{:S(2)}) %collective-permute-start.2) | collective-permute-done | bytes 131104 | tf_op jit(solution)/shard_map/ppermute | solution.py:86
  129.6 2.0 dynamic_update_slice.23
  131.6 0.0 collective-permute-done.3
  131.6 2.0 dynamic_update_slice.24
  133.7 2.0 dynamic_update_slice.25
  135.7 2.0 dynamic_update_slice.26
  137.7 0.0 collective-permute-done.6
  137.7 2.0 dynamic_update_slice.27
  139.8 0.2 convert_element_type.90
  140.0 1.2 copy.26
  141.2 0.0 copy-start.3
  141.2 0.0 copy-start.6
  141.3 1.1 multiply_convert_fusion
  142.4 0.0 all-reduce.2.cloned.1.call-update
  142.4 0.8 multiply_reduce_fusion
  143.2 0.0 all-gather.2.cloned.1.call-done
  143.3 1.8 copy.25
  145.1 0.0 copy-start.4
  145.1 1.6 copy.19
  146.6 4.2 %all-to-all-start = ((bf16[1,32,8,2048]{3,1,0,2:T(8,128)(2,1)}), bf16[1,32,8,2048]{3,1,0,2:T(8,128)(2,1)}, u32[]{:S(2)}, u32[]{:S(2)}) async-start(bf16[1,32,8,2048]{3,1,0,2:T(8,128)(2,1)} %copy.19), calls=%async_computation | async-start | bytes 2097152 | tf_op jit(solution)/shard_map/all_to_all | solution.py:114
  150.9 25.5 %all-reduce.2.cloned.1.call-done = bf16[32,16384]{1,0:T(8,128)(2,1)} async-done(((bf16[32,16384]{1,0:T(8,128)(2,1)}), bf16[32,16384]{1,0:T(8,128)(2,1)}) %all-reduce.2.cloned.1.call-update) | async-done | bytes 1048592 | tf_op jit(solution)/shard_map/psum | solution.py:99
  176.4 1.5 convert_multiply_fusion
  177.9 1.2 copy.28
  179.1 1.9 convolution_bitcast_fusion
  181.0 0.3 fusion.21
  181.4 0.3 copy.29
  181.7 0.1 multiply_convert_fusion.1
  181.8 1.6 broadcast_in_dim.49
  183.3 5.6 %all-to-all-start.2 = ((bf16[1,32,8,4096]{3,1,0,2:T(8,128)(2,1)}), bf16[1,32,8,4096]{3,1,0,2:T(8,128)(2,1)S(1)}, u32[]{:S(2)}, u32[]{:S(2)}) async-start(bf16[1,32,8,4096]{3,1,0,2:T(8,128)(2,1)} %broadcast_in_dim.49), calls=%async_computation.2 | async-start | bytes 4194304 | tf_op jit(solution)/shard_map/all_to_all | solution.py:121
  189.0 0.3 reduce-scatter.2.cloned.1.call-start
  189.3 0.2 compare_reduce_fusion
  189.5 0.1 copy.18
  189.6 2.2 broadcast_in_dim.18
  191.8 4.1 %copy.23 = pred[512,8,4,256]{3,1,2,0:T(8,128)(4,1)} copy(pred[512,8,4,256]{3,2,1,0:T(4,128)(4,1)S(1)} %bitcast.85) | data formatting | bytes 8388608
  195.9 40.6 %all-to-all-done.2 = bf16[1,32,8,4096]{3,1,0,2:T(8,128)(2,1)S(1)} async-done(((bf16[1,32,8,4096]{3,1,0,2:T(8,128)(2,1)}), bf16[1,32,8,4096]{3,1,0,2:T(8,128)(2,1)S(1)}, u32[]{:S(2)}, u32[]{:S(2)}) %all-to-all-start.2) | async-done | bytes 2097184 | tf_op jit(solution)/shard_map/all_to_all | solution.py:121
  236.5 10.0 %bitcast_convert_fusion.clone.7 = bf16[2048,4096]{1,0:T(8,128)(2,1)} fusion(bf16[1,32,8,4096]{3,1,0,2:T(8,128)(2,1)S(1)} %all-to-all-done.2, bf16[1,32,8,2048]{3,1,0,2:T(8,128)(2,1)} %all-to-all-done), kind=kOutput, calls=%fused_computation.clone.clone.clone.clone.clone.2 | convolution fusion | flops 4303355904 | bytes 19922944 | tf_op jit(solution)/shard_map/bpgr,bpgc->rc/dot_general | solution.py:123
  246.4 25.2 %fusion.5 = bf16[1024,2048]{1,0:T(8,128)(2,1)} fusion(pred[4096,1024]{1,0:T(8,128)(4,1)} %bitcast.91, bf16[4096,1024]{1,0:T(8,128)(2,1)} %param.18, bf16[2048,4096]{1,0:T(8,128)(2,1)} %bitcast_convert_fusion.clone.7), kind=kOutput, calls=%fused_computation.7 | convolution fusion | flops 17186160640 | bytes 33554432 | tf_op jit(solution)/shard_map/dot_general | solution.py:137
  271.6 0.0 reduce-scatter.2.cloned.1.call-update
  271.6 43.6 %reduce-scatter.2.cloned.1.call-done = bf16[256,2048]{1,0:T(8,128)(2,1)} async-done(((bf16[1024,2048]{1,0:T(8,128)(2,1)}), bf16[256,2048]{1,0:T(8,128)(2,1)}) %reduce-scatter.2.cloned.1.call-update) | async-done | bytes 1048592 | tf_op jit(solution)/shard_map/reduce_scatter | solution.py:136
  (20 shorter events, 0.1 us)
Async XLA Ops:
  6.5 174.5 %copy-start = (bf16[512,512]{1,0:T(8,128)(2,1)S(1)}, bf16[512,512]{1,0:T(8,128)(2,1)}, u32[]{:S(2)}) copy-start(bf16[512,512]{1,0:T(8,128)(2,1)} %param.13) | copy-start | bytes 1572868
  8.7 1.5 copy-start.2
  10.2 55.7 %all-to-all-start.1 = ((bf16[1,32,8,4096]{3,1,0,2:T(8,128)(2,1)}), bf16[1,32,8,4096]{3,1,0,2:T(8,128)(2,1)}, u32[]{:S(2)}, u32[]{:S(2)}) async-start(bf16[1,32,8,4096]{3,1,0,2:T(8,128)(2,1)} %broadcast_multiply_fusion), calls=%async_computation.1 | async-start | bytes 4194304 | tf_op jit(solution)/shard_map/all_to_all | solution.py:74
  17.5 125.7 %all-gather.2.cloned.1.call-start = ((), (), s32[]{:S(2)}) async-start(), calls=%async_computation.4 | async-start | bytes 1310720 | tf_op jit(solution)/shard_map/all_gather | solution.py:112
  80.3 11.0 %collective-permute-start.1 = (bf16[1,1,32,1,2048]{4,0,2,3,1:T(2,128)(2,1)S(1)}, bf16[1,1,32,1,2048]{4,0,2,3,1:T(2,128)(2,1)S(1)}, u32[]{:S(2)}, u32[]{:S(2)}) collective-permute-start(bf16[1,1,32,1,2048]{4,0,2,3,1:T(2,128)(2,1)S(1)} %get-tuple-element.12), channel_id=1, source_target_pairs={{0,8},{4,12},{8,16},{12,20},{16,24},{20,28},{24,0},{28,4},{1,9},{5... | collective-permute-start | bytes 393224 | tf_op jit(solution)/shard_map/ppermute | solution.py:86
  80.3 21.2 %collective-permute-start = (bf16[1,1,32,1,2048]{4,0,2,3,1:T(2,128)(2,1)S(1)}, bf16[1,1,32,1,2048]{4,0,2,3,1:T(2,128)(2,1)S(1)}, u32[]{:S(2)}, u32[]{:S(2)}) collective-permute-start(bf16[1,1,32,1,2048]{4,0,2,3,1:T(2,128)(2,1)S(1)} %get-tuple-element.13), channel_id=1, source_target_pairs={{0,4},{4,8},{8,12},{12,16},{16,20},{20,24},{24,28},{28,0},{1,5},{5... | collective-permute-start | bytes 393224 | tf_op jit(solution)/shard_map/ppermute | solution.py:86
  81.8 94.6 %all-reduce.2.cloned.1.call-start = ((), (), s32[]{:S(2)}) async-start(), calls=%async_computation.5 | async-start | bytes 2097152 | tf_op jit(solution)/shard_map/psum | solution.py:99
  81.9 55.8 %collective-permute-start.6 = (bf16[1,1,32,1,2048]{4,0,2,3,1:T(2,128)(2,1)}, bf16[1,1,32,1,2048]{4,0,2,3,1:T(2,128)(2,1)S(1)}, u32[]{:S(2)}, u32[]{:S(2)}) collective-permute-start(bf16[1,1,32,1,2048]{4,0,2,3,1:T(2,128)(2,1)} %get-tuple-element.7), channel_id=1, source_target_pairs={{0,28},{4,0},{8,4},{12,8},{16,12},{20,16},{24,20},{28,24},{1,29},{... | collective-permute-start | bytes 393224 | tf_op jit(solution)/shard_map/ppermute | solution.py:86
  85.2 50.4 %collective-permute-start.5 = (bf16[1,1,32,1,2048]{4,0,2,3,1:T(2,128)(2,1)}, bf16[1,1,32,1,2048]{4,0,2,3,1:T(2,128)(2,1)S(1)}, u32[]{:S(2)}, u32[]{:S(2)}) collective-permute-start(bf16[1,1,32,1,2048]{4,0,2,3,1:T(2,128)(2,1)} %get-tuple-element.8), channel_id=1, source_target_pairs={{0,24},{4,28},{8,0},{12,4},{16,8},{20,12},{24,16},{28,20},{1,25},{... | collective-permute-start | bytes 393224 | tf_op jit(solution)/shard_map/ppermute | solution.py:86
  87.3 46.4 %collective-permute-start.4 = (bf16[1,1,32,1,2048]{4,0,2,3,1:T(2,128)(2,1)}, bf16[1,1,32,1,2048]{4,0,2,3,1:T(2,128)(2,1)S(1)}, u32[]{:S(2)}, u32[]{:S(2)}) collective-permute-start(bf16[1,1,32,1,2048]{4,0,2,3,1:T(2,128)(2,1)} %get-tuple-element.9), channel_id=1, source_target_pairs={{0,20},{4,24},{8,28},{12,0},{16,4},{20,8},{24,12},{28,16},{1,21},{... | collective-permute-start | bytes 393224 | tf_op jit(solution)/shard_map/ppermute | solution.py:86
  91.2 40.4 %collective-permute-start.3 = (bf16[1,1,32,1,2048]{4,0,2,3,1:T(2,128)(2,1)}, bf16[1,1,32,1,2048]{4,0,2,3,1:T(2,128)(2,1)S(1)}, u32[]{:S(2)}, u32[]{:S(2)}) collective-permute-start(bf16[1,1,32,1,2048]{4,0,2,3,1:T(2,128)(2,1)} %get-tuple-element.10), channel_id=1, source_target_pairs={{0,16},{4,20},{8,24},{12,28},{16,0},{20,4},{24,8},{28,12},{1,17},{... | collective-permute-start | bytes 393224 | tf_op jit(solution)/shard_map/ppermute | solution.py:86
  101.5 28.1 %collective-permute-start.2 = (bf16[1,1,32,1,2048]{4,0,2,3,1:T(2,128)(2,1)}, bf16[1,1,32,1,2048]{4,0,2,3,1:T(2,128)(2,1)S(1)}, u32[]{:S(2)}, u32[]{:S(2)}) collective-permute-start(bf16[1,1,32,1,2048]{4,0,2,3,1:T(2,128)(2,1)} %get-tuple-element.11), channel_id=1, source_target_pairs={{0,12},{4,16},{8,20},{12,24},{16,28},{20,0},{24,4},{28,8},{1,13},{... | collective-permute-start | bytes 393224 | tf_op jit(solution)/shard_map/ppermute | solution.py:86
  141.2 1.2 copy-start.3
  141.2 1.2 copy-start.6
  145.1 31.3 %copy-start.4 = (f32[16384]{0:T(1024)S(1)}, f32[16384]{0:T(1024)}, u32[]{:S(2)}) copy-start(f32[16384]{0:T(1024)} %param.16) | copy-start | bytes 196612
  146.6 35.1 %all-to-all-start = ((bf16[1,32,8,2048]{3,1,0,2:T(8,128)(2,1)}), bf16[1,32,8,2048]{3,1,0,2:T(8,128)(2,1)}, u32[]{:S(2)}, u32[]{:S(2)}) async-start(bf16[1,32,8,2048]{3,1,0,2:T(8,128)(2,1)} %copy.19), calls=%async_computation | async-start | bytes 2097152 | tf_op jit(solution)/shard_map/all_to_all | solution.py:114
  183.3 5.9 %copy-start.5 = (s32[4,16]{1,0:T(4,128)S(1)}, s32[4,16]{1,0:T(4,128)}, u32[]{:S(2)}) copy-start(s32[4,16]{1,0:T(4,128)} %param.19) | copy-start | bytes 772
  183.3 53.1 %all-to-all-start.2 = ((bf16[1,32,8,4096]{3,1,0,2:T(8,128)(2,1)}), bf16[1,32,8,4096]{3,1,0,2:T(8,128)(2,1)S(1)}, u32[]{:S(2)}, u32[]{:S(2)}) async-start(bf16[1,32,8,4096]{3,1,0,2:T(8,128)(2,1)} %broadcast_in_dim.49), calls=%async_computation.2 | async-start | bytes 4194304 | tf_op jit(solution)/shard_map/all_to_all | solution.py:121
  189.0 126.2 %reduce-scatter.2.cloned.1.call-start = ((), (), s32[]{:S(2)}) async-start(), calls=%async_computation.6 | async-start | bytes 5242880 | tf_op jit(solution)/shard_map/reduce_scatter | solution.py:136
  271.6 43.6 %copy-start.1 = (bf16[512,512]{1,0:T(8,128)(2,1)S(1)}, bf16[512,512]{1,0:T(8,128)(2,1)}, u32[]{:S(2)}) copy-start(bf16[512,512]{1,0:T(8,128)(2,1)} %param.13) | copy-start | bytes 1572868
Sparse Core Ops, SparseCore 0:
  81.9 17.1 all-gather.1
  142.5 33.8 all-reduce.1
  271.7 43.4 reduce-scatter.1
